TPU v7x, 512 devices: a whole 4x8x8 slice. The times are simulated.
512 devices in a mesh: elem: 32 (over z, y_lo), mode: 16 (over x, y_hi, core).
Axes of the slice: x: 4, y: 8 (y_hi: 2, y_lo: 4; y = y_hi * 4 + y_lo), z: 8, core: 2. Of those that a mesh axis runs over, the one named last changes fastest.
Arguments:
- modal_history: float32 [4096, 512], P('elem', 'mode'), may hold values from -6 to 6
- stress_modes: float32 [512, 6144], P('mode', 'elem'), may hold values from -0.5 to 0.5
Outputs:
- stress_spectrum: float32 [6144, 2, 2048], P(('elem', 'mode'))
All inputs are finite; a program needn't handle non-finite values.
Results may differ from a plain program's by a relative error of at most 0.00007.
Values sent between devices are 32-bit elements; how exact they have to be, the bound alone decides.
No kernel may reach another device: no remote copies, remote signals or barrier semaphores. Data moves between devices by JAX's collectives and lax.ppermute only.
A program may use at most 64 MiB of HBM per device.

v0:
```python
import math
import jax
import jax.numpy as jnp
from jax import lax
from jax.sharding import PartitionSpec as P

highest = lax.Precision.HIGHEST


def spectra(signal):
    columns = signal.shape[0]
    radix = 64
    halved = radix // 2
    blocked = signal.reshape(columns, radix, radix)
    counter = jnp.arange(radix, dtype=jnp.int32)
    products = counter[:, None] * counter[None, :]
    small_angle = (products % radix).astype(jnp.float32) * (2.0 * math.pi / radix)
    cosine_small = jnp.cos(small_angle)
    sine_small = jnp.sin(small_angle)
    twist_angle = (products % (radix * radix)).astype(jnp.float32) * (
        2.0 * math.pi / (radix * radix)
    )
    twist_cos = jnp.cos(twist_angle)
    twist_sin = jnp.sin(twist_angle)
    first_real = jnp.einsum("cab,ak->cbk", blocked, cosine_small, precision=highest)
    first_imag = -jnp.einsum("cab,ak->cbk", blocked, sine_small, precision=highest)
    turned_real = first_real * twist_cos + first_imag * twist_sin
    turned_imag = first_imag * twist_cos - first_real * twist_sin
    cosine_half = cosine_small[:, :halved]
    sine_half = sine_small[:, :halved]
    final_real = jnp.einsum(
        "cbk,bj->cjk", turned_real, cosine_half, precision=highest
    ) + jnp.einsum("cbk,bj->cjk", turned_imag, sine_half, precision=highest)
    final_imag = jnp.einsum(
        "cbk,bj->cjk", turned_imag, cosine_half, precision=highest
    ) - jnp.einsum("cbk,bj->cjk", turned_real, sine_half, precision=highest)
    stacked = jnp.stack([final_real, final_imag], axis=1) * (1.0 / radix)
    return stacked.reshape(columns, 2, halved * radix)


def per_device(modal_history, stress_modes):
    elem_count = lax.axis_size("elem")
    mode_count = lax.axis_size("mode")
    local_steps = modal_history.shape[0]
    partial_value = jnp.einsum(
        "mp,tm->pt",
        lax.all_gather(stress_modes, "elem", axis=1, tiled=True),
        modal_history,
        precision=highest,
        preferred_element_type=jnp.float32,
    )
    owned_width = partial_value.shape[0] // (elem_count * mode_count)
    reordered = partial_value.reshape(elem_count, mode_count, owned_width, local_steps)
    reordered = reordered.transpose(1, 0, 2, 3).reshape(
        mode_count * elem_count * owned_width, local_steps
    )
    summed = lax.psum_scatter(reordered, "mode", scatter_dimension=0, tiled=True)
    stress = lax.all_to_all(summed, "elem", split_axis=0, concat_axis=1, tiled=True)
    return spectra(stress)


def solution(mesh):
    placed = (P("elem", "mode"), P("mode", "elem"))
    return jax.shard_map(
        per_device,
        mesh=mesh,
        in_specs=placed,
        out_specs=P(("elem", "mode"), None, None),
        check_vma=False,
    )
```

profile of v0, /device:TPU:2, one launch (start us, length us, event | category | flops | bytes accessed | tf_op | source)
XLA Modules:
  0.0 250.8 jit_solution(8755520814195808711)
XLA Ops:
  6.5 0.0 copy-start
  6.5 0.0 reduce-scatter.2.cloned.1.call-start
  6.5 95.5 %all-gather = f32[32,192,32]{1,2,0:T(8,128)S(1)} all-gather(f32[1,192,32]{1,2,0:T(8,128)} %bitcast.31), channel_id=1, replica_groups=mesh['elem'=32,'mode'=16] {'elem'}, dimensions={0}, use_global_device_ids=true | all-gather | bytes 811008 | tf_op jit(solution)/shard_map/all_gather | solution.py:47
  102.0 0.6 copy.19
  102.6 1.3 reshape.58
  103.9 0.0 copy-done
  103.9 6.2 %fusion.32 = f32[6144,128]{1,0:T(8,128)S(1)} fusion(f32[6144,32]{0,1:T(8,128)} %reshape.58, f32[128,32]{0,1:T(8,128)S(1)} %copy-done), kind=kOutput, calls=%fused_computation.44 | convolution fusion | flops 301989888 | bytes 3948544 | tf_op jit(solution)/shard_map/mp,tm->pt/dot_general | solution.py:45
  110.1 2.1 reshape.54
  112.2 4.6 %copy.20 = f32[16,32,12,128]{3,2,1,0:T(8,128)} copy(f32[16,32,12,128]{3,2,0,1:T(8,128)} %bitcast.29) | data formatting | bytes 6291456 | tf_op jit(solution)/shard_map/transpose | solution.py:54
  116.8 4.6 %reshape.55 = f32[6144,128]{1,0:T(8,128)} reshape(f32[16,32,12,128]{3,2,1,0:T(8,128)} %copy.20) | data formatting | bytes 6291456 | tf_op jit(solution)/shard_map/reshape | solution.py:54
  121.4 0.0 reduce-scatter.2.cloned.1.call-update
  121.4 94.8 %reduce-scatter.2.cloned.1.call-done = f32[384,128]{1,0:T(8,128)} async-done(((f32[6144,128]{1,0:T(8,128)}), f32[384,128]{1,0:T(8,128)}) %reduce-scatter.2.cloned.1.call-update) | async-done | bytes 196624 | tf_op jit(solution)/shard_map/reduce_scatter | solution.py:57
  216.2 1.6 all_to_all.12
  217.9 9.7 %all-to-all-start = ((f32[32,12,128]{2,1,0:T(8,128)}), f32[32,12,128]{2,1,0:T(8,128)S(1)}, u32[]{:S(2)}, u32[]{:S(2)}) async-start(f32[32,12,128]{2,1,0:T(8,128)} %all_to_all.12), calls=%async_computation.1 | async-start | bytes 524288 | tf_op jit(solution)/shard_map/all_to_all | solution.py:58
  227.6 0.1 fusion.19
  227.7 0.1 copy.24
  227.8 0.1 fusion.18
  228.0 0.1 copy.27
  228.1 0.2 fusion.21
  228.2 0.1 fusion.20
  228.4 11.2 %all-to-all-done = f32[32,12,128]{2,1,0:T(8,128)S(1)} async-done(((f32[32,12,128]{2,1,0:T(8,128)}), f32[32,12,128]{2,1,0:T(8,128)S(1)}, u32[]{:S(2)}, u32[]{:S(2)}) %all-to-all-start) | async-done | bytes 196640 | tf_op jit(solution)/shard_map/all_to_all | solution.py:58
  239.5 0.1 copy.21
  239.6 0.1 reshape.56
  239.7 0.8 convolution_negate_fusion
  240.6 0.8 fusion.9
  241.4 0.4 fusion.2
  241.7 0.4 fusion.3
  242.1 0.4 fusion.1
  242.5 0.1 stack.9
  242.6 0.4 fusion
  242.9 0.1 stack.10
  243.1 0.8 copy.28
  (1 shorter events, 0.0 us)
Async XLA Ops:
  6.5 97.4 %copy-start = (f32[128,32]{0,1:T(8,128)S(1)}, f32[128,32]{0,1:T(8,128)}, u32[]{:S(2)}) copy-start(f32[128,32]{0,1:T(8,128)} %param.2) | copy-start | bytes 49156
  6.5 209.7 %reduce-scatter.2.cloned.1.call-start = ((), (), s32[]{:S(2)}) async-start(), calls=%async_computation.2 | async-start | bytes 3342336 | tf_op jit(solution)/shard_map/reduce_scatter | solution.py:57
  217.9 21.7 %all-to-all-start = ((f32[32,12,128]{2,1,0:T(8,128)}), f32[32,12,128]{2,1,0:T(8,128)S(1)}, u32[]{:S(2)}, u32[]{:S(2)}) async-start(f32[32,12,128]{2,1,0:T(8,128)} %all_to_all.12), calls=%async_computation.1 | async-start | bytes 524288 | tf_op jit(solution)/shard_map/all_to_all | solution.py:58
Sparse Core Ops, SparseCore 0:
  121.6 94.6 reduce-scatter.1
where the time goes:
time: 251 us
  waiting for transfers between devices  106 us (42%)
  blocking collectives  95.5 us (38%)
  local copies, waits for them, and re-layouts  16.2 us (6%)
  between operations  13.5 us (5%)
  starting transfers between devices  9.72 us (4%)
  matrix products  9.24 us (4%)
    all_gather x1, blocking collectives, per_device(): lax.all_gather(stress_modes, 'elem', axis=1, tiled=True)  95.5 us
    reduce_scatter x1, waiting for transfers between devices, per_device(): lax.psum_scatter(reordered, 'mode', scatter_dimension=0, tiled=True)  94.8 us
    all_to_all x1, waiting for transfers between devices, per_device(): lax.all_to_all(summed, 'elem', split_axis=0, concat_axis=1, tiled=True)  11.2 us
    all_to_all x1, starting transfers between devices, per_device(): lax.all_to_all(summed, 'elem', split_axis=0, concat_axis=1, tiled=True)  9.72 us
    dot_general x1, matrix products, per_device(): jnp.einsum('mp,tm->pt', lax.all_gather(stress_modes, 'elem', axis=1, tile...  6.19 us
  transfers between devices with their start and end apart: 2, of which 2 were waited for; matrix products, arithmetic and copies ran while one was open for 0% of the time, Pallas kernels for 0%

commit v1 on v0

--- a/solution.py
+++ b/solution.py
@@ -42,9 +42,19 @@
     elem_count = lax.axis_size("elem")
     mode_count = lax.axis_size("mode")
     local_steps = modal_history.shape[0]
+
+    def set_copies(page, ax_name="elem"):
+        x_next = jnp.concatenate(
+            lax.all_to_all(
+                jnp.stack([page for _ in range(lax.axis_size(ax_name))], 0), ax_name, 0, 0
+            ),
+            1,
+        )
+        return x_next
+
     partial_value = jnp.einsum(
         "mp,tm->pt",
-        lax.all_gather(stress_modes, "elem", axis=1, tiled=True),
+        set_copies(stress_modes),
         modal_history,
         precision=highest,
         preferred_element_type=jnp.float32,

time: 251 us -> 210 us (0.84)
  blocking collectives: 95.5 us -> 40.9 us
  local copies, waits for them, and re-layouts: 16.2 us -> 29.9 us
  matrix products: 9.24 us -> 5.8 us
  waiting for transfers between devices: 106 us -> 109 us
    all_gather x1 -> x0, blocking collectives: 95.5 us -> none  [per_device(): lax.all_gather(stress_modes, 'elem', axis=1, tiled=True)]
    all_to_all x0 -> x1, blocking collectives: none -> 40.9 us  [set_copies(): lax.all_to_all(jnp.stack([page for _ in range(lax.axis_size(ax_name))], 0...]
    dot_general x0 -> x2, local copies, waits for them, and re-layouts: none -> 17.4 us  [per_device(): jnp.einsum('mp,tm->pt', set_copies(stress_modes), modal_history, precisio...]
    dot_general x1, matrix products: 6.19 us -> 2.75 us  [per_device(): jnp.einsum('mp,tm->pt', set_copies(stress_modes), modal_history, precisio...]
    reduce_scatter x1, waiting for transfers between devices: 94.8 us -> 97.7 us  [per_device(): lax.psum_scatter(reordered, 'mode', scatter_dimension=0, tiled=True)]
where the time goes in v1:
time: 210 us; the launch traced here: 209 us
  waiting for transfers between devices  109 us (52%)
  blocking collectives  40.9 us (19%)
  local copies, waits for them, and re-layouts  29.9 us (14%)
  between operations  13.5 us (6%)
  starting transfers between devices  9.89 us (5%)
  matrix products  5.8 us (3%)
    reduce_scatter x1, waiting for transfers between devices, per_device(): lax.psum_scatter(reordered, 'mode', scatter_dimension=0, tiled=True)  97.7 us
    all_to_all x1, blocking collectives, set_copies(): lax.all_to_all(jnp.stack([page for _ in range(lax.axis_size(ax_name))], 0...  40.9 us
    dot_general x2, local copies, waits for them, and re-layouts, per_device(): jnp.einsum('mp,tm->pt', set_copies(stress_modes), modal_history, precisio...  17.4 us
    all_to_all x1, waiting for transfers between devices, per_device(): lax.all_to_all(summed, 'elem', split_axis=0, concat_axis=1, tiled=True)  11 us
    all_to_all x1, starting transfers between devices, per_device(): lax.all_to_all(summed, 'elem', split_axis=0, concat_axis=1, tiled=True)  9.89 us
    reshape x1, local copies, waits for them, and re-layouts, per_device(): reordered.transpose(1, 0, 2, 3)  4.59 us
  transfers between devices with their start and end apart: 2, of which 2 were waited for; matrix products, arithmetic and copies ran while one was open for 0% of the time, Pallas kernels for 0%

profile of v1, /device:TPU:2, one launch (start us, length us, event | category | flops | bytes accessed | tf_op | source)
XLA Modules:
  0.0 209.4 jit_solution(10778998492722708715)
XLA Ops:
  6.5 0.0 copy-start
  6.5 0.0 reduce-scatter.2.cloned.1.call-start
  6.5 0.9 stack.8
  7.4 40.9 %all_to_all.21 = f32[32,32,192]{2,1,0:T(8,128)S(1)} all-to-all(f32[32,32,192]{2,1,0:T(8,128)S(1)} %stack.8), channel_id=1, replica_groups=mesh['elem'=32,'mode'=16] {'elem'}, dimensions={0} | all-to-all | bytes 1572864 | tf_op jit(solution)/shard_map/all_to_all | solution.py:48
  48.4 0.6 copy.20
  49.0 0.4 reshape.62
  49.4 10.6 %reshape.70 = f32[32,16,12,32]{2,1,0,3:T(8,128)} reshape(f32[6144,32]{0,1:T(8,128)S(1)} %bitcast.34) | data formatting | bytes 1572864 | tf_op jit(solution)/shard_map/mp,tm->pt/dot_general | solution.py:55
  60.0 6.9 %copy.22 = f32[32,16,12,32]{3,1,2,0:T(8,128)S(1)} copy(f32[32,16,12,32]{2,1,0,3:T(8,128)} %reshape.70) | data formatting | bytes 1572864 | tf_op jit(solution)/shard_map/mp,tm->pt/dot_general | solution.py:55
  66.8 0.0 copy-done
  66.8 2.7 %convolution_bitcast_fusion = f32[16,32,12,128]{3,0,2,1:T(8,128)S(1)} fusion(f32[32,16,12,32]{3,1,2,0:T(8,128)S(1)} %copy.22, f32[128,32]{0,1:T(8,128)S(1)} %copy-done), kind=kOutput, calls=%fused_computation | convolution fusion | flops 301989888 | bytes 3948544 | tf_op jit(solution)/shard_map/mp,tm->pt/dot_general | solution.py:55
  69.6 3.0 %copy.23 = f32[16,32,12,128]{3,2,1,0:T(8,128)} copy(f32[16,32,12,128]{3,0,2,1:T(8,128)S(1)} %convolution_bitcast_fusion) | data formatting | bytes 6291456 | tf_op jit(solution)/shard_map/transpose | solution.py:64
  72.6 4.6 %reshape.63 = f32[6144,128]{1,0:T(8,128)} reshape(f32[16,32,12,128]{3,2,1,0:T(8,128)} %copy.23) | data formatting | bytes 6291456 | tf_op jit(solution)/shard_map/reshape | solution.py:64
  77.2 0.0 reduce-scatter.2.cloned.1.call-update
  77.2 97.7 %reduce-scatter.2.cloned.1.call-done = f32[384,128]{1,0:T(8,128)} async-done(((f32[6144,128]{1,0:T(8,128)}), f32[384,128]{1,0:T(8,128)}) %reduce-scatter.2.cloned.1.call-update) | async-done | bytes 196624 | tf_op jit(solution)/shard_map/reduce_scatter | solution.py:67
  174.9 1.6 all_to_all.16
  176.5 9.9 %all-to-all-start.1 = ((f32[32,12,128]{2,1,0:T(8,128)}), f32[32,12,128]{2,1,0:T(8,128)S(1)}, u32[]{:S(2)}, u32[]{:S(2)}) async-start(f32[32,12,128]{2,1,0:T(8,128)} %all_to_all.16), calls=%async_computation.2 | async-start | bytes 524288 | tf_op jit(solution)/shard_map/all_to_all | solution.py:68
  186.4 0.1 fusion.20
  186.6 0.1 copy.27
  186.6 0.1 fusion.19
  186.8 0.1 copy.30
  186.9 0.2 fusion.22
  187.0 0.1 fusion.21
  187.2 11.0 %all-to-all-done.1 = f32[32,12,128]{2,1,0:T(8,128)S(1)} async-done(((f32[32,12,128]{2,1,0:T(8,128)}), f32[32,12,128]{2,1,0:T(8,128)S(1)}, u32[]{:S(2)}, u32[]{:S(2)}) %all-to-all-start.1) | async-done | bytes 196640 | tf_op jit(solution)/shard_map/all_to_all | solution.py:68
  198.2 0.1 copy.24
  198.2 0.1 reshape.64
  198.4 0.8 convolution_negate_fusion
  199.2 0.8 fusion.9
  200.0 0.4 fusion.2
  200.4 0.4 fusion.3
  200.7 0.4 fusion.1
  201.1 0.1 stack.9
  201.2 0.4 fusion
  201.6 0.1 stack.10
  201.7 0.8 copy.31
  (1 shorter events, 0.0 us)
Async XLA Ops:
  6.5 60.3 %copy-start = (f32[128,32]{0,1:T(8,128)S(1)}, f32[128,32]{0,1:T(8,128)}, u32[]{:S(2)}) copy-start(f32[128,32]{0,1:T(8,128)} %param.2) | copy-start | bytes 49156
  6.5 168.3 %reduce-scatter.2.cloned.1.call-start = ((), (), s32[]{:S(2)}) async-start(), calls=%async_computation.3 | async-start | bytes 3342336 | tf_op jit(solution)/shard_map/reduce_scatter | solution.py:67
  176.5 21.7 %all-to-all-start.1 = ((f32[32,12,128]{2,1,0:T(8,128)}), f32[32,12,128]{2,1,0:T(8,128)S(1)}, u32[]{:S(2)}, u32[]{:S(2)}) async-start(f32[32,12,128]{2,1,0:T(8,128)} %all_to_all.16), calls=%async_computation.2 | async-start | bytes 524288 | tf_op jit(solution)/shard_map/all_to_all | solution.py:68
Sparse Core Ops, SparseCore 0:
  77.3 97.5 reduce-scatter.1
